TPU v7x, 256 devices: a whole 4x4x8 slice. The times are simulated.
256 devices in a mesh: dom: 64 (over z, x, core), grp: 4 (over y).
Axes of the slice: x: 4, y: 4, z: 8, core: 2. Of those that a mesh axis runs over, the one named last changes fastest.
Arguments:
- blocks: bfloat16 [12288, 6, 128, 128], P(('dom', 'grp')), may hold values from -0.21875 to 0.21875
- local_cols: int32 [12288, 4], P(('dom', 'grp')), may hold values from 0 to 191
- remote_refs: int32 [12288, 2], P(('dom', 'grp')), may hold values from 0 to 191
- send_blocks: int32 [64, 4, 64, 3], P('dom', 'grp'), may hold values from 0 to 47
- send_counts: int32 [64, 4, 64], P('dom', 'grp'), may hold values from 0 to 3
- probes: bfloat16 [64, 1572864], P(None, ('dom', 'grp')), may hold values from -6 to 6
Outputs:
- moments: float32 [3, 1572864], P(None, ('dom', 'grp'))
All inputs are finite; a program needn't handle non-finite values.
Results may differ from a plain program's by a relative error of at most 0.00064.
Values may be sent and summed in bfloat16 or wider, within the bound.
No kernel may reach another device: no remote copies, remote signals or barrier semaphores. Data moves between devices by JAX's collectives and lax.ppermute only.
A program may use at most 64 MiB of HBM per device.

v0:
```python
import math
import jax
import jax.numpy as jnp
from jax import lax
from jax.sharding import PartitionSpec as P

PROBES = 64
LOCAL = 4
KMOM = 256


def jackson(order, total):
    angle = math.pi / (total + 1)
    return (
        (total - order + 1) * math.cos(order * angle) + math.sin(order * angle) / math.tan(angle)
    ) / (total + 1)


def send_boundary(own, send_list, live):
    outgoing = jnp.take(own, send_list, axis=1)
    outgoing = jnp.where(live[None, :, :, None], outgoing, jnp.zeros_like(outgoing))
    received = lax.all_to_all(outgoing, "dom", split_axis=1, concat_axis=1, tiled=True)
    return received.reshape(own.shape[0], -1, own.shape[2])


def on_device(blocks, local_cols, remote_refs, send_blocks, send_counts, probes):
    rows_here = blocks.shape[0]
    size_block = blocks.shape[2]
    probe_count = probes.shape[0]
    local_blocks = blocks[:, :LOCAL]
    remote_blocks = blocks[:, LOCAL:]
    send_list = send_blocks[0, 0]
    slot_index = jnp.arange(send_list.shape[1], dtype=jnp.int32)
    live = slot_index[None, :] < send_counts[0, 0][:, None]

    def local_part(own):
        panel_all = lax.all_gather(own, "grp", axis=1, tiled=True)
        picked = jnp.take(panel_all, local_cols, axis=1)
        return jnp.einsum(
            "rjab,prjb->pra", local_blocks, picked, preferred_element_type=jnp.float32
        )

    def remote_part(received):
        picked = jnp.take(received, remote_refs, axis=1)
        return jnp.einsum(
            "rjab,prjb->pra", remote_blocks, picked, preferred_element_type=jnp.float32
        )

    def apply_op(field):
        own = field.reshape(probe_count, rows_here, size_block)
        local_sum = local_part(own)
        received = send_boundary(own, send_list, live)
        result = local_sum + remote_part(received)
        return result.reshape(probe_count, rows_here * size_block)

    first = apply_op(probes).astype(jnp.bfloat16)
    base = probes.astype(jnp.float32)
    second = 2.0 * apply_op(first) - base
    norm = 1.0 / math.sqrt(PROBES)
    moment_zero = jackson(0, KMOM) * norm * jnp.sum(base * base, axis=0)
    moment_one = 2.0 * jackson(1, KMOM) * norm * jnp.sum(base * first.astype(jnp.float32), axis=0)
    moment_two = 2.0 * jackson(2, KMOM) * norm * jnp.sum(base * second, axis=0)
    return jnp.stack([moment_zero, moment_one, moment_two], axis=0)


def solution(mesh):
    in_specs = (
        P(("dom", "grp"), None, None, None),
        P(("dom", "grp"), None),
        P(("dom", "grp"), None),
        P("dom", "grp", None, None),
        P("dom", "grp", None),
        P(None, ("dom", "grp")),
    )
    out_specs = P(None, ("dom", "grp"))
    return jax.shard_map(
        on_device, mesh=mesh, in_specs=in_specs, out_specs=out_specs, check_vma=False
    )
```

profile of v0, /device:TPU:16, one launch (start us, length us, event | category | flops | bytes accessed | tf_op | source)
XLA Modules:
  0.0 208.0 jit_solution(10266669360849559524)
XLA Ops:
  6.5 0.7 compare_select_fusion
  7.2 0.7 compare_and_fusion.1
  7.9 1.3 copy_bitcast_fusion
  9.4 0.1 reshape.151
  9.5 0.1 copy.51
  9.6 0.7 iota_compare_fusion
  10.4 2.7 %gather_fusion.1 = bf16[192,64,128]{2,1,0:T(8,128)(2,1)} fusion(bf16[64,48,128]{2,0,1:T(8,128)(2,1)S(1)} %copy_bitcast_fusion, s32[1024]{0:T(1024)S(1)} %pad_clamp_fusion.1), kind=kCustom, calls=%fused_computation.1.clone | custom fusion | bytes 6292224 | tf_op jit(solution)/shard_map/jit(_take)/gather | solution.py:20
  13.1 3.3 %bitcast_select_fusion.1 = bf16[64,64,3,128]{3,0,2,1:T(8,128)(2,1)} fusion(bf16[64,3,64,128]{3,2,1,0:T(8,128)(2,1)} %bitcast.78, pred[64,3]{1,0:T(8,128)(4,1)S(1)} %copy.51, pred[64,3]{1,0:T(8,128)(4,1)S(1)} %iota_compare_fusion), kind=kLoop, calls=%fused_computation.12 | loop fusion | flops 3145728 | bytes 6291840 | tf_op jit(solution)/shard_map/jit(_where)/select_n | solution.py:21
  16.5 12.1 %all-to-all-start = ((bf16[64,64,3,128]{3,0,2,1:T(8,128)(2,1)}), bf16[64,64,3,128]{3,0,2,1:T(8,128)(2,1)S(1)}, u32[]{:S(2)}, u32[]{:S(2)}) async-start(bf16[64,64,3,128]{3,0,2,1:T(8,128)(2,1)} %bitcast_select_fusion.1), calls=%async_computation | async-start | bytes 6291456 | tf_op jit(solution)/shard_map/all_to_all | solution.py:22
  28.6 0.7 all-gather.3.cloned.1.call-update
  29.4 0.1 reshape.155
  29.6 0.1 reshape.147
  29.7 0.1 copy.47
  29.9 0.1 copy.50
  30.0 43.3 %all-gather.3.cloned.1.call-done = bf16[64,192,128]{2,0,1:T(8,128)(2,1)} async-done(((bf16[64,48,128]{2,0,1:T(8,128)(2,1)}), bf16[64,192,128]{2,0,1:T(8,128)(2,1)}) %all-gather.3.cloned.1.call-update) | async-done | bytes 3145744 | tf_op jit(solution)/shard_map/all_gather | solution.py:37
  73.3 4.7 %gather_fusion = bf16[192,64,128]{2,1,0:T(8,128)(2,1)} fusion(bf16[64,192,128]{2,0,1:T(8,128)(2,1)} %all-gather.3.cloned.1.call-done, s32[1024]{0:T(1024)S(1)} %pad_clamp_fusion.2), kind=kCustom, calls=%fused_computation.clone | custom fusion | bytes 6292224 | tf_op jit(solution)/shard_map/jit(_take)/gather | solution.py:38
  77.9 7.2 %fusion.2 = f32[48,64,128,1]{2,1,3,0:T(8,128)} fusion(bf16[48,6,128,128]{3,2,1,0:T(8,128)(2,1)} %param.12, bf16[48,4,64,128]{3,2,1,0:T(8,128)(2,1)} %bitcast.83, pred[48,4]{1,0:T(8,128)(4,1)S(1)} %copy.47), kind=kOutput, calls=%fused_computation.8 | convolution fusion | flops 404226048 | bytes 11010240 | tf_op jit(solution)/shard_map/rjab,prjb->pra/dot_general | solution.py:39
  85.2 17.2 %all-to-all-done = bf16[64,64,3,128]{3,0,2,1:T(8,128)(2,1)S(1)} async-done(((bf16[64,64,3,128]{3,0,2,1:T(8,128)(2,1)}), bf16[64,64,3,128]{3,0,2,1:T(8,128)(2,1)S(1)}, u32[]{:S(2)}, u32[]{:S(2)}) %all-to-all-start) | async-done | bytes 3145760 | tf_op jit(solution)/shard_map/all_to_all | solution.py:22
  102.4 1.9 gather_fusion.2
  104.3 4.1 %fusion.36 = bf16[64,48,128]{2,0,1:T(8,128)(2,1)S(1)} fusion(bf16[48,6,128,128]{3,2,1,0:T(8,128)(2,1)} %param.12, bf16[48,2,64,128]{3,2,1,0:T(8,128)(2,1)} %bitcast.84, pred[48,2]{1,0:T(8,128)(4,1)S(1)} %copy.50, f32[48,64,128,1]{2,1,3,0:T(8,128)} %fusion.2), kind=kOutput, calls=%fused_computation.43 | convolution fusion | flops 202899456 | bytes 7077984 | tf_op jit(solution)/shard_map/rjab,prjb->pra/dot_general | solution.py:45
  108.4 2.7 %gather_fusion.4 = bf16[192,64,128]{2,1,0:T(8,128)(2,1)} fusion(bf16[64,48,128]{2,0,1:T(8,128)(2,1)S(1)} %fusion.36, s32[1024]{0:T(1024)S(1)} %pad_clamp_fusion.1), kind=kCustom, calls=%fused_computation.4.clone | custom fusion | bytes 6292224 | tf_op jit(solution)/shard_map/jit(_take)/gather | solution.py:20
  111.2 3.3 %bitcast_select_fusion = bf16[64,64,3,128]{3,0,2,1:T(8,128)(2,1)} fusion(bf16[64,3,64,128]{3,2,1,0:T(8,128)(2,1)} %bitcast.77, pred[64,3]{1,0:T(8,128)(4,1)S(1)} %copy.51, pred[64,3]{1,0:T(8,128)(4,1)S(1)} %iota_compare_fusion), kind=kLoop, calls=%fused_computation.10 | loop fusion | flops 3145728 | bytes 6291840 | tf_op jit(solution)/shard_map/jit(_where)/select_n | solution.py:21
  114.5 5.3 %all-to-all-start.1 = ((bf16[64,64,3,128]{3,0,2,1:T(8,128)(2,1)}), bf16[64,64,3,128]{3,0,2,1:T(8,128)(2,1)S(1)}, u32[]{:S(2)}, u32[]{:S(2)}) async-start(bf16[64,64,3,128]{3,0,2,1:T(8,128)(2,1)} %bitcast_select_fusion), calls=%async_computation.1 | async-start | bytes 6291456 | tf_op jit(solution)/shard_map/all_to_all | solution.py:22
  119.9 0.7 all-gather.5.cloned.1.call-update
  120.6 44.0 %all-gather.5.cloned.1.call-done = bf16[64,192,128]{2,0,1:T(8,128)(2,1)} async-done(((bf16[64,48,128]{2,0,1:T(8,128)(2,1)}), bf16[64,192,128]{2,0,1:T(8,128)(2,1)}) %all-gather.5.cloned.1.call-update) | async-done | bytes 3145744 | tf_op jit(solution)/shard_map/all_gather | solution.py:37
  164.6 4.6 %gather_fusion.3 = bf16[192,64,128]{2,1,0:T(8,128)(2,1)} fusion(bf16[64,192,128]{2,0,1:T(8,128)(2,1)} %all-gather.5.cloned.1.call-done, s32[1024]{0:T(1024)S(1)} %pad_clamp_fusion.2), kind=kCustom, calls=%fused_computation.3.clone | custom fusion | bytes 6292224 | tf_op jit(solution)/shard_map/jit(_take)/gather | solution.py:38
  169.2 7.2 %fusion = f32[48,64,128,1]{2,1,3,0:T(8,128)} fusion(bf16[48,6,128,128]{3,2,1,0:T(8,128)(2,1)} %param.12, bf16[48,4,64,128]{3,2,1,0:T(8,128)(2,1)} %bitcast.82, pred[48,4]{1,0:T(8,128)(4,1)S(1)} %copy.47), kind=kOutput, calls=%fused_computation.6 | convolution fusion | flops 404226048 | bytes 11010240 | tf_op jit(solution)/shard_map/rjab,prjb->pra/dot_general | solution.py:39
  176.4 17.2 %all-to-all-done.1 = bf16[64,64,3,128]{3,0,2,1:T(8,128)(2,1)S(1)} async-done(((bf16[64,64,3,128]{3,0,2,1:T(8,128)(2,1)}), bf16[64,64,3,128]{3,0,2,1:T(8,128)(2,1)S(1)}, u32[]{:S(2)}, u32[]{:S(2)}) %all-to-all-start.1) | async-done | bytes 3145760 | tf_op jit(solution)/shard_map/all_to_all | solution.py:22
  193.7 1.9 gather_fusion.5
  195.6 4.2 %fusion.18 = f32[48,8,8,128]{3,2,1,0:T(8,128)S(1)} fusion(f32[48,64,128,1]{2,1,3,0:T(8,128)} %fusion, bf16[48,6,128,128]{3,2,1,0:T(8,128)(2,1)} %param.12, bf16[48,2,64,128]{3,2,1,0:T(8,128)(2,1)} %bitcast.81, pred[48,2]{1,0:T(8,128)(4,1)S(1)} %copy.50), kind=kOutput, calls=%fused_computation.31 | convolution fusion | flops 202899456 | bytes 7864416 | tf_op jit(solution)/shard_map/rjab,prjb->pra/dot_general | solution.py:45
  199.8 0.6 fusion.14
  200.5 0.7 pad_maximum_fusion
  (26 shorter events, 0.4 us)
Async XLA Ops:
  9.3 3.9 %copy-start = (bf16[64,48,128]{2,0,1:T(8,128)(2,1)}, bf16[64,48,128]{2,0,1:T(8,128)(2,1)S(1)}, u32[]{:S(2)}) copy-start(bf16[64,48,128]{2,0,1:T(8,128)(2,1)S(1)} %copy_bitcast_fusion) | copy-start | bytes 2359300
  16.5 12.8 %copy-start.5 = (s32[48,2]{0,1:T(2,128)S(1)}, s32[48,2]{0,1:T(2,128)}, u32[]{:S(2)}) copy-start(s32[48,2]{0,1:T(2,128)} %param.14) | copy-start | bytes 1156
  16.5 13.1 %copy-start.4 = (s32[48,4]{0,1:T(4,128)S(1)}, s32[48,4]{0,1:T(4,128)}, u32[]{:S(2)}) copy-start(s32[48,4]{0,1:T(4,128)} %param.13) | copy-start | bytes 2308
  16.5 85.9 %all-to-all-start = ((bf16[64,64,3,128]{3,0,2,1:T(8,128)(2,1)}), bf16[64,64,3,128]{3,0,2,1:T(8,128)(2,1)S(1)}, u32[]{:S(2)}, u32[]{:S(2)}) async-start(bf16[64,64,3,128]{3,0,2,1:T(8,128)(2,1)} %bitcast_select_fusion.1), calls=%async_computation | async-start | bytes 6291456 | tf_op jit(solution)/shard_map/all_to_all | solution.py:22
  28.5 44.8 %all-gather.3.cloned.1.call-start = ((), (), s32[]{:S(2)}) async-start(), calls=%async_computation.2 | async-start | bytes 3932160 | tf_op jit(solution)/shard_map/all_gather | solution.py:37
  108.4 2.8 %copy-start.1 = (bf16[64,48,128]{2,0,1:T(8,128)(2,1)}, bf16[64,48,128]{2,0,1:T(8,128)(2,1)S(1)}, u32[]{:S(2)}) copy-start(bf16[64,48,128]{2,0,1:T(8,128)(2,1)S(1)} %fusion.36) | copy-start | bytes 2359300
  114.5 79.1 %all-to-all-start.1 = ((bf16[64,64,3,128]{3,0,2,1:T(8,128)(2,1)}), bf16[64,64,3,128]{3,0,2,1:T(8,128)(2,1)S(1)}, u32[]{:S(2)}, u32[]{:S(2)}) async-start(bf16[64,64,3,128]{3,0,2,1:T(8,128)(2,1)} %bitcast_select_fusion), calls=%async_computation.1 | async-start | bytes 6291456 | tf_op jit(solution)/shard_map/all_to_all | solution.py:22
  119.8 44.8 %all-gather.5.cloned.1.call-start = ((), (), s32[]{:S(2)}) async-start(), calls=%async_computation.3 | async-start | bytes 3932160 | tf_op jit(solution)/shard_map/all_gather | solution.py:37
  195.6 4.2 %copy-start.2 = (bf16[64,48,128]{2,0,1:T(8,128)(2,1)S(1)}, bf16[64,48,128]{2,0,1:T(8,128)(2,1)}, u32[]{:S(2)}) copy-start(bf16[64,48,128]{2,0,1:T(8,128)(2,1)} %copy-done.1) | copy-start | bytes 2359300
  195.6 4.2 %copy-start.3 = (bf16[64,6144]{1,0:T(8,128)(2,1)S(1)}, bf16[64,6144]{1,0:T(8,128)(2,1)}, u32[]{:S(2)}) copy-start(bf16[64,6144]{1,0:T(8,128)(2,1)} %param.17) | copy-start | bytes 2359300
Sparse Core Ops, SparseCore 0:
  31.2 42.0 all-gather.2
  122.4 42.0 all-gather.4
where the time goes:
time: 208 us
  waiting for transfers between devices  123 us (59%)
  matrix products  22.7 us (11%)
  local copies, waits for them, and re-layouts  21 us (10%)
  starting transfers between devices  17.4 us (8%)
  between operations  13.6 us (7%)
  other arithmetic  10.1 us (5%)
    all_gather x2, waiting for transfers between devices, local_part(): panel_all = lax.all_gather(own, 'grp', axis=1, tiled=True)  87.3 us
    all_to_all x2, waiting for transfers between devices, send_boundary(): lax.all_to_all(outgoing, 'dom', split_axis=1, concat_axis=1, tiled=True)  34.4 us
    all_to_all x2, starting transfers between devices, send_boundary(): lax.all_to_all(outgoing, 'dom', split_axis=1, concat_axis=1, tiled=True)  17.3 us
    dot_general x2, matrix products, local_part(): jnp.einsum('rjab,prjb->pra', local_blocks, picked, preferred_element_type...  14.5 us
    gather x2, local copies, waits for them, and re-layouts, local_part(): picked = jnp.take(panel_all, local_cols, axis=1)  9.29 us
    dot_general x2, matrix products, remote_part(): jnp.einsum('rjab,prjb->pra', remote_blocks, picked, preferred_element_typ...  8.29 us
    select_n x2, other arithmetic, send_boundary(): jnp.where(live[None, :, :, None], outgoing, jnp.zeros_like(outgoing))  6.68 us
    gather x2, local copies, waits for them, and re-layouts, send_boundary(): outgoing = jnp.take(own, send_list, axis=1)  5.5 us
  transfers between devices with their start and end apart: 4, of which 4 were waited for; matrix products, arithmetic and copies ran while one was open for 12% of the time, Pallas kernels for 0%

commit v1 on v0

--- a/solution.py
+++ b/solution.py
@@ -34,7 +34,14 @@
     live = slot_index[None, :] < send_counts[0, 0][:, None]
 
     def local_part(own):
-        panel_all = lax.all_gather(own, "grp", axis=1, tiled=True)
+
+        def lots_all_find(vector):
+            x_now = lax.axis_size("grp")
+            row_out = jnp.stack([vector] * x_now, axis=0)
+            carry_out = jnp.concatenate(lax.all_to_all(row_out, "grp", 0, 0), axis=1)
+            return carry_out
+
+        panel_all = lots_all_find(own)
         picked = jnp.take(panel_all, local_cols, axis=1)
         return jnp.einsum(
             "rjab,prjb->pra", local_blocks, picked, preferred_element_type=jnp.float32

time: 208 us -> 271 us (1.30); the launches traced: 208 us -> 268 us
  waiting for transfers between devices: 123 us -> 168 us
  starting transfers between devices: 17.4 us -> 33.5 us
  local copies, waits for them, and re-layouts: 21 us -> 36.8 us
  between operations: 13.6 us -> 0.23 us
    all_gather x2 -> x0, waiting for transfers between devices: 87.3 us -> none  [local_part(): panel_all = lax.all_gather(own, 'grp', axis=1, tiled=True)]
    all_to_all x2, waiting for transfers between devices: 34.4 us -> 113 us  [send_boundary(): lax.all_to_all(outgoing, 'dom', split_axis=1, concat_axis=1, tiled=True)]
    all_to_all x0 -> x2, waiting for transfers between devices: none -> 54.1 us  [lots_all_find(): carry_out = jnp.concatenate(lax.all_to_all(row_out, 'grp', 0, 0), axis=1)]
    all_to_all x0 -> x2, starting transfers between devices: none -> 14.3 us  [lots_all_find(): carry_out = jnp.concatenate(lax.all_to_all(row_out, 'grp', 0, 0), axis=1)]
    all_to_all x0 -> x2, local copies, waits for them, and re-layouts: none -> 5.7 us  [lots_all_find(): carry_out = jnp.concatenate(lax.all_to_all(row_out, 'grp', 0, 0), axis=1)]
    another operation x0 -> x3, local copies, waits for them, and re-layouts: none -> 4.4 us  [lots_all_find(): row_out = jnp.stack([vector] * x_now, axis=0)]
    reshape x1 -> x2, local copies, waits for them, and re-layouts: 1.34 us -> 5.71 us  [lots_all_find(): carry_out = jnp.concatenate(lax.all_to_all(row_out, 'grp', 0, 0), axis=1)]
  transfers between devices with their start and end apart: 4 -> 4, of which waited for: 4 -> 4; matrix products, arithmetic and copies ran while one was open for 12% -> 17% of each run, Pallas kernels for 0% -> 0%
where the time goes in v1:
time: 271 us; the launch traced here: 268 us
  waiting for transfers between devices  168 us (62%)
  local copies, waits for them, and re-layouts  36.8 us (14%)
  starting transfers between devices  33.5 us (12%)
  matrix products  21.8 us (8%)
  other arithmetic  8.13 us (3%)
    all_to_all x2, waiting for transfers between devices, send_boundary(): lax.all_to_all(outgoing, 'dom', split_axis=1, concat_axis=1, tiled=True)  113 us
    all_to_all x2, waiting for transfers between devices, lots_all_find(): carry_out = jnp.concatenate(lax.all_to_all(row_out, 'grp', 0, 0), axis=1)  54.1 us
    all_to_all x2, starting transfers between devices, send_boundary(): lax.all_to_all(outgoing, 'dom', split_axis=1, concat_axis=1, tiled=True)  19.1 us
    dot_general x2, matrix products, local_part(): jnp.einsum('rjab,prjb->pra', local_blocks, picked, preferred_element_type...  14.5 us
    all_to_all x2, starting transfers between devices, lots_all_find(): carry_out = jnp.concatenate(lax.all_to_all(row_out, 'grp', 0, 0), axis=1)  14.3 us
    gather x2, local copies, waits for them, and re-layouts, local_part(): picked = jnp.take(panel_all, local_cols, axis=1)  7.38 us
    dot_general x2, matrix products, remote_part(): jnp.einsum('rjab,prjb->pra', remote_blocks, picked, preferred_element_typ...  7.3 us
    select_n x2, other arithmetic, send_boundary(): jnp.where(live[None, :, :, None], outgoing, jnp.zeros_like(outgoing))  6.7 us
  transfers between devices with their start and end apart: 4, of which 4 were waited for; matrix products, arithmetic and copies ran while one was open for 17% of the time, Pallas kernels for 0%

profile of v1, /device:TPU:16, one launch (start us, length us, event | category | flops | bytes accessed | tf_op | source)
XLA Modules:
  0.0 268.0 jit_solution(9184374917667646811)
XLA Ops:
  0.0 1.3 copy.81
  1.3 2.1 stack.12
  3.4 6.8 %all-to-all-start = ((bf16[4,64,48,128]{3,2,1,0:T(8,128)(2,1)}), bf16[4,64,48,128]{3,2,1,0:T(8,128)(2,1)}, u32[]{:S(2)}, u32[]{:S(2)}) async-start(bf16[4,64,48,128]{3,2,1,0:T(8,128)(2,1)} %stack.12), calls=%async_computation | async-start | bytes 6291456 | tf_op jit(solution)/shard_map/all_to_all | solution.py:41
  10.2 0.1 reshape.168
  10.5 0.2 copy_bitcast_fusion
  10.8 2.7 %gather_fusion.1 = bf16[192,64,128]{2,1,0:T(8,128)(2,1)} fusion(bf16[64,48,128]{2,0,1:T(8,128)(2,1)S(1)} %copy_bitcast_fusion, s32[1024]{0:T(1024)S(1)} %pad_clamp_fusion.1), kind=kCustom, calls=%fused_computation.1.clone | custom fusion | bytes 6292224 | tf_op jit(solution)/shard_map/jit(_take)/gather | solution.py:20
  13.6 3.4 %bitcast_select_fusion.1 = bf16[64,64,3,128]{3,0,2,1:T(8,128)(2,1)} fusion(bf16[64,3,64,128]{3,2,1,0:T(8,128)(2,1)} %bitcast.86, pred[64,3]{1,0:T(8,128)(4,1)S(1)} %copy.58, pred[64,3]{1,0:T(8,128)(4,1)S(1)} %iota_compare_fusion), kind=kLoop, calls=%fused_computation.12 | loop fusion | flops 3145728 | bytes 6291840 | tf_op jit(solution)/shard_map/jit(_where)/select_n | solution.py:21
  16.9 26.4 %all-to-all-done = bf16[4,64,48,128]{3,2,1,0:T(8,128)(2,1)} async-done(((bf16[4,64,48,128]{3,2,1,0:T(8,128)(2,1)}), bf16[4,64,48,128]{3,2,1,0:T(8,128)(2,1)}, u32[]{:S(2)}, u32[]{:S(2)}) %all-to-all-start) | async-done | bytes 3145760 | tf_op jit(solution)/shard_map/all_to_all | solution.py:41
  43.3 12.3 %all-to-all-start.1 = ((bf16[64,64,3,128]{3,0,2,1:T(8,128)(2,1)}), bf16[64,64,3,128]{3,0,2,1:T(8,128)(2,1)}, u32[]{:S(2)}, u32[]{:S(2)}) async-start(bf16[64,64,3,128]{3,0,2,1:T(8,128)(2,1)} %bitcast_select_fusion.1), calls=%async_computation.1 | async-start | bytes 6291456 | tf_op jit(solution)/shard_map/all_to_all | solution.py:22
  56.3 2.8 %copy.54 = bf16[4,64,48,128]{3,2,0,1:T(8,128)(2,1)S(1)} copy(bf16[4,64,48,128]{3,2,1,0:T(8,128)(2,1)} %all-to-all-done) | data formatting | bytes 6291456 | tf_op jit(solution)/shard_map/all_to_all | solution.py:41
  59.2 2.0 copy.56
  61.2 2.7 %gather_fusion = bf16[192,64,128]{2,1,0:T(8,128)(2,1)} fusion(bf16[64,192,128]{2,0,1:T(8,128)(2,1)S(1)} %copy.56, s32[1024]{0:T(1024)S(1)} %pad_clamp_fusion.2), kind=kCustom, calls=%fused_computation.clone | custom fusion | bytes 6292224 | tf_op jit(solution)/shard_map/jit(_take)/gather | solution.py:45
  63.9 7.2 %fusion.2 = f32[48,64,128,1]{2,1,3,0:T(8,128)} fusion(bf16[48,6,128,128]{3,2,1,0:T(8,128)(2,1)} %param.12, bf16[48,4,64,128]{3,2,1,0:T(8,128)(2,1)} %bitcast.92, pred[48,4]{1,0:T(8,128)(4,1)S(1)} %copy.53), kind=kOutput, calls=%fused_computation.8 | convolution fusion | flops 404226048 | bytes 11010240 | tf_op jit(solution)/shard_map/rjab,prjb->pra/dot_general | solution.py:46
  71.2 58.1 %all-to-all-done.1 = bf16[64,64,3,128]{3,0,2,1:T(8,128)(2,1)} async-done(((bf16[64,64,3,128]{3,0,2,1:T(8,128)(2,1)}), bf16[64,64,3,128]{3,0,2,1:T(8,128)(2,1)}, u32[]{:S(2)}, u32[]{:S(2)}) %all-to-all-start.1) | async-done | bytes 3145760 | tf_op jit(solution)/shard_map/all_to_all | solution.py:22
  129.3 2.7 %gather_fusion.2 = bf16[96,64,128]{2,1,0:T(8,128)(2,1)S(1)} fusion(bf16[64,192,128]{2,0,1:T(8,128)(2,1)} %bitcast.10, s32[1024]{0:T(1024)S(1)} %pad_clamp_fusion), kind=kCustom, calls=%fused_computation.2.clone | custom fusion | bytes 3146112 | tf_op jit(solution)/shard_map/jit(_take)/gather | solution.py:51
  132.1 3.6 %fusion.36 = bf16[64,48,128]{2,0,1:T(8,128)(2,1)S(1)} fusion(bf16[48,6,128,128]{3,2,1,0:T(8,128)(2,1)} %param.12, bf16[48,2,64,128]{3,2,1,0:T(8,128)(2,1)S(1)} %bitcast.94, pred[48,2]{1,0:T(8,128)(4,1)S(1)} %copy.57, f32[48,64,128,1]{2,1,3,0:T(8,128)} %fusion.2), kind=kOutput, calls=%fused_computation.43 | convolution fusion | flops 202899456 | bytes 7077984 | tf_op jit(solution)/shard_map/rjab,prjb->pra/dot_general | solution.py:52
  135.7 0.5 copy.64
  136.2 2.1 stack.13
  138.3 7.6 %all-to-all-start.2 = ((bf16[4,64,48,128]{3,2,1,0:T(8,128)(2,1)}), bf16[4,64,48,128]{3,2,1,0:T(8,128)(2,1)}, u32[]{:S(2)}, u32[]{:S(2)}) async-start(bf16[4,64,48,128]{3,2,1,0:T(8,128)(2,1)} %stack.13), calls=%async_computation.2 | async-start | bytes 6291456 | tf_op jit(solution)/shard_map/all_to_all | solution.py:41
  145.9 2.7 %gather_fusion.4 = bf16[192,64,128]{2,1,0:T(8,128)(2,1)} fusion(bf16[64,48,128]{2,0,1:T(8,128)(2,1)S(1)} %fusion.36, s32[1024]{0:T(1024)S(1)} %pad_clamp_fusion.1), kind=kCustom, calls=%fused_computation.4.clone | custom fusion | bytes 6292224 | tf_op jit(solution)/shard_map/jit(_take)/gather | solution.py:20
  148.6 3.3 %bitcast_select_fusion = bf16[64,64,3,128]{3,0,2,1:T(8,128)(2,1)} fusion(bf16[64,3,64,128]{3,2,1,0:T(8,128)(2,1)} %bitcast.85, pred[64,3]{1,0:T(8,128)(4,1)S(1)} %copy.58, pred[64,3]{1,0:T(8,128)(4,1)S(1)} %iota_compare_fusion), kind=kLoop, calls=%fused_computation.10 | loop fusion | flops 3145728 | bytes 6291840 | tf_op jit(solution)/shard_map/jit(_where)/select_n | solution.py:21
  151.9 27.7 %all-to-all-done.2 = bf16[4,64,48,128]{3,2,1,0:T(8,128)(2,1)} async-done(((bf16[4,64,48,128]{3,2,1,0:T(8,128)(2,1)}), bf16[4,64,48,128]{3,2,1,0:T(8,128)(2,1)}, u32[]{:S(2)}, u32[]{:S(2)}) %all-to-all-start.2) | async-done | bytes 3145760 | tf_op jit(solution)/shard_map/all_to_all | solution.py:41
  179.6 6.8 %all-to-all-start.3 = ((bf16[64,64,3,128]{3,0,2,1:T(8,128)(2,1)}), bf16[64,64,3,128]{3,0,2,1:T(8,128)(2,1)}, u32[]{:S(2)}, u32[]{:S(2)}) async-start(bf16[64,64,3,128]{3,0,2,1:T(8,128)(2,1)} %bitcast_select_fusion), calls=%async_computation.3 | async-start | bytes 6291456 | tf_op jit(solution)/shard_map/all_to_all | solution.py:22
  186.5 2.8 %copy.65 = bf16[4,64,48,128]{3,2,0,1:T(8,128)(2,1)S(1)} copy(bf16[4,64,48,128]{3,2,1,0:T(8,128)(2,1)} %all-to-all-done.2) | data formatting | bytes 6291456 | tf_op jit(solution)/shard_map/all_to_all | solution.py:41
  189.3 3.7 %copy.67 = bf16[64,192,128]{2,0,1:T(8,128)(2,1)} copy(bf16[64,192,128]{2,1,0:T(8,128)(2,1)S(1)} %bitcast.88) | data formatting | bytes 6291456 | tf_op jit(solution)/shard_map/reshape | solution.py:41
  193.0 4.6 %gather_fusion.3 = bf16[192,64,128]{2,1,0:T(8,128)(2,1)} fusion(bf16[64,192,128]{2,0,1:T(8,128)(2,1)} %copy.67, s32[1024]{0:T(1024)S(1)} %pad_clamp_fusion.2), kind=kCustom, calls=%fused_computation.3.clone | custom fusion | bytes 6292224 | tf_op jit(solution)/shard_map/jit(_take)/gather | solution.py:45
  197.6 7.2 %fusion = f32[48,64,128,1]{2,1,3,0:T(8,128)} fusion(bf16[48,6,128,128]{3,2,1,0:T(8,128)(2,1)} %param.12, bf16[48,4,64,128]{3,2,1,0:T(8,128)(2,1)} %bitcast.91, pred[48,4]{1,0:T(8,128)(4,1)S(1)} %copy.53), kind=kOutput, calls=%fused_computation.6 | convolution fusion | flops 404226048 | bytes 11010240 | tf_op jit(solution)/shard_map/rjab,prjb->pra/dot_general | solution.py:46
  204.9 55.3 %all-to-all-done.3 = bf16[64,64,3,128]{3,0,2,1:T(8,128)(2,1)} async-done(((bf16[64,64,3,128]{3,0,2,1:T(8,128)(2,1)}), bf16[64,64,3,128]{3,0,2,1:T(8,128)(2,1)}, u32[]{:S(2)}, u32[]{:S(2)}) %all-to-all-start.3) | async-done | bytes 3145760 | tf_op jit(solution)/shard_map/all_to_all | solution.py:22
  260.2 2.7 %gather_fusion.5 = bf16[96,64,128]{2,1,0:T(8,128)(2,1)S(1)} fusion(bf16[64,192,128]{2,0,1:T(8,128)(2,1)} %bitcast.25, s32[1024]{0:T(1024)S(1)} %pad_clamp_fusion), kind=kCustom, calls=%fused_computation.5.clone | custom fusion | bytes 3146112 | tf_op jit(solution)/shard_map/jit(_take)/gather | solution.py:51
  263.0 3.7 %fusion.18 = f32[48,8,8,128]{3,2,1,0:T(8,128)S(1)} fusion(f32[48,64,128,1]{2,1,3,0:T(8,128)} %fusion, bf16[48,6,128,128]{3,2,1,0:T(8,128)(2,1)} %param.12, bf16[48,2,64,128]{3,2,1,0:T(8,128)(2,1)S(1)} %bitcast.90, pred[48,2]{1,0:T(8,128)(4,1)S(1)} %copy.57), kind=kOutput, calls=%fused_computation.31 | convolution fusion | flops 202899456 | bytes 7864416 | tf_op jit(solution)/shard_map/rjab,prjb->pra/dot_general | solution.py:52
  266.7 0.6 fusion.14
  267.3 0.7 pad_maximum_fusion
  (32 shorter events, 1.0 us)
Async XLA Ops:
  3.4 6.8 %copy-start.3 = (s32[1,1,64,3]{2,1,3,0:T(1,128)S(1)}, s32[1,1,64,3]{2,1,3,0:T(1,128)}, u32[]{:S(2)}) copy-start(s32[1,1,64,3]{2,1,3,0:T(1,128)} %param.15) | copy-start | bytes 2308
  3.4 7.2 %copy-start = (bf16[64,6144]{1,0:T(8,128)(2,1)S(1)}, bf16[64,6144]{1,0:T(8,128)(2,1)}, u32[]{:S(2)}) copy-start(bf16[64,6144]{1,0:T(8,128)(2,1)} %param.17) | copy-start | bytes 2359300
  3.4 39.9 %all-to-all-start = ((bf16[4,64,48,128]{3,2,1,0:T(8,128)(2,1)}), bf16[4,64,48,128]{3,2,1,0:T(8,128)(2,1)}, u32[]{:S(2)}, u32[]{:S(2)}) async-start(bf16[4,64,48,128]{3,2,1,0:T(8,128)(2,1)} %stack.12), calls=%async_computation | async-start | bytes 6291456 | tf_op jit(solution)/shard_map/all_to_all | solution.py:41
  10.8 2.7 %copy-start.5 = (s32[1,1,64]{2,1,0:T(1,128)S(1)}, s32[1,1,64]{2,1,0:T(1,128)}, u32[]{:S(2)}) copy-start(s32[1,1,64]{2,1,0:T(1,128)} %param.16) | copy-start | bytes 772
  16.9 38.7 %copy-start.4 = (s32[48,2]{0,1:T(2,128)S(1)}, s32[48,2]{0,1:T(2,128)}, u32[]{:S(2)}) copy-start(s32[48,2]{0,1:T(2,128)} %param.14) | copy-start | bytes 1156
  16.9 38.9 %copy-start.2 = (s32[48,4]{0,1:T(4,128)S(1)}, s32[48,4]{0,1:T(4,128)}, u32[]{:S(2)}) copy-start(s32[48,4]{0,1:T(4,128)} %param.13) | copy-start | bytes 2308
  43.3 86.0 %all-to-all-start.1 = ((bf16[64,64,3,128]{3,0,2,1:T(8,128)(2,1)}), bf16[64,64,3,128]{3,0,2,1:T(8,128)(2,1)}, u32[]{:S(2)}, u32[]{:S(2)}) async-start(bf16[64,64,3,128]{3,0,2,1:T(8,128)(2,1)} %bitcast_select_fusion.1), calls=%async_computation.1 | async-start | bytes 6291456 | tf_op jit(solution)/shard_map/all_to_all | solution.py:22
  138.3 41.4 %all-to-all-start.2 = ((bf16[4,64,48,128]{3,2,1,0:T(8,128)(2,1)}), bf16[4,64,48,128]{3,2,1,0:T(8,128)(2,1)}, u32[]{:S(2)}, u32[]{:S(2)}) async-start(bf16[4,64,48,128]{3,2,1,0:T(8,128)(2,1)} %stack.13), calls=%async_computation.2 | async-start | bytes 6291456 | tf_op jit(solution)/shard_map/all_to_all | solution.py:41
  179.6 80.6 %all-to-all-start.3 = ((bf16[64,64,3,128]{3,0,2,1:T(8,128)(2,1)}), bf16[64,64,3,128]{3,0,2,1:T(8,128)(2,1)}, u32[]{:S(2)}, u32[]{:S(2)}) async-start(bf16[64,64,3,128]{3,0,2,1:T(8,128)(2,1)} %bitcast_select_fusion), calls=%async_computation.3 | async-start | bytes 6291456 | tf_op jit(solution)/shard_map/all_to_all | solution.py:22
  262.9 3.7 %copy-start.1 = (bf16[64,6144]{1,0:T(8,128)(2,1)S(1)}, bf16[64,6144]{1,0:T(8,128)(2,1)}, u32[]{:S(2)}) copy-start(bf16[64,6144]{1,0:T(8,128)(2,1)} %param.17) | copy-start | bytes 2359300
